TPU v7x, 32 devices: a whole 2x2x4 slice. The times are simulated.
32 devices in a mesh: bin: 4 (over x, core), fsdp: 8 (over z, y).
Axes of the slice: x: 2, y: 2, z: 4, core: 2. Of those that a mesh axis runs over, the one named last changes fastest.
Arguments:
- latents: bfloat16 [4, 16, 256, 1152], P('bin', 'fsdp'), may hold values from -6 to 6
- cond: float32 [4, 1152], P('bin'), may hold values from -6 to 6
- live: int32 [4, 8], P('bin', 'fsdp'), may hold values from 1 to 2, 12 in all within a row
- w_ada: bfloat16 [1152, 6912], P(None, 'fsdp'), may hold values from -0.375 to 0.375
- b_ada: bfloat16 [6912], P('fsdp'), may hold values from -3 to 3
- w_qkv: bfloat16 [1152, 3456], P('fsdp'), may hold values from -0.1875 to 0.1875
- b_qv: bfloat16 [2304], P('fsdp'), may hold values from -3 to 3
- w_proj: bfloat16 [1152, 1152], P('fsdp'), may hold values from -0.5 to 0.5
- b_proj: bfloat16 [1152], P('fsdp'), may hold values from -3 to 3
- w_fc1: bfloat16 [1152, 4608], P('fsdp'), may hold values from -0.1875 to 0.1875
- b_fc1: bfloat16 [4608], P('fsdp'), may hold values from -3 to 3
- w_fc2: bfloat16 [4608, 1152], P('fsdp'), may hold values from -0.09375 to 0.09375
- b_fc2: bfloat16 [1152], P('fsdp'), may hold values from -3 to 3
- cotangent: bfloat16 [4, 16, 256, 1152], P('bin', 'fsdp'), may hold values from -6 to 6
Outputs:
- block_out: bfloat16 [4, 16, 256, 1152], P('bin', 'fsdp')
- latents_grad: float32 [4, 16, 256, 1152], P('bin', 'fsdp')
- cond_grad: float32 [4, 1152], P('bin')
- w_ada_grad: float32 [1152, 6912], P(None, 'fsdp')
- b_ada_grad: float32 [6912], P('fsdp')
- w_qkv_grad: float32 [1152, 3456], P('fsdp')
- b_qv_grad: float32 [2304], P('fsdp')
- w_proj_grad: float32 [1152, 1152], P('fsdp')
- b_proj_grad: float32 [1152], P('fsdp')
- w_fc1_grad: float32 [1152, 4608], P('fsdp')
- b_fc1_grad: float32 [4608], P('fsdp')
- w_fc2_grad: float32 [4608, 1152], P('fsdp')
- b_fc2_grad: float32 [1152], P('fsdp')
Inputs may be any that keep to these rules, and one draw needn't show every extreme that they name: The counts of one bin's devices sum to 12; every bin has a device with 2 live images; a device's live images are its first slots.
All inputs are finite; a program needn't handle non-finite values.
Results may differ from a plain program's by a relative error of at most 0.015.
The roundings to bfloat16 on the way count: a program that leaves them out, or rounds other values in their place, can miss the bound.
Values may be sent and summed in bfloat16 or wider, within the bound.
A program may use at most 256 MiB of HBM per device.

v0:
```python
import jax
import jax.numpy as jnp
from jax import lax
from jax.sharding import PartitionSpec as P

HEAD_DIM = 72


def layer_norm(field):
    center = field - jnp.mean(field, axis=-1, keepdims=True)
    return center * lax.rsqrt(jnp.mean(center * center, axis=-1, keepdims=True) + 1e-06)


def gelu_tanh(field):
    return (
        0.5
        * field
        * (1.0 + jnp.tanh(0.7978845608028654 * (field + 0.044715 * field * field * field)))
    )


def modulate(field, shift_vec, scale_vec):
    return layer_norm(field) * (1.0 + scale_vec) + shift_vec


def pair_scores(query_block, key_block):
    return jnp.einsum(
        "gqhd,gkhd->ghqk", query_block, key_block, preferred_element_type=jnp.float32
    ) * HEAD_DIM ** (-0.5)


def attend_pair(group_item):
    query_block, key_block, value_block = group_item
    scores = pair_scores(query_block, key_block)
    highest = jnp.max(scores, axis=-1, keepdims=True)
    exp_scores = jnp.exp(scores - highest)
    totals = jnp.sum(exp_scores, axis=-1, keepdims=True)
    attn_probs = (exp_scores / totals).astype(jnp.bfloat16)
    attended = jnp.einsum(
        "ghqk,gkhd->gqhd", attn_probs, value_block, preferred_element_type=jnp.float32
    )
    return (attended, (highest + jnp.log(totals))[..., 0])


def attend_back(group_item):
    query_block, key_block, value_block, log_total, grad_att = group_item
    scores = pair_scores(query_block, key_block)
    attn_probs = jnp.exp(scores - log_total[..., None])
    grad_probs = jnp.einsum(
        "gqhd,gkhd->ghqk", grad_att, value_block, preferred_element_type=jnp.float32
    )
    row_terms = jnp.sum(attn_probs * grad_probs, axis=-1, keepdims=True)
    grad_scores = (attn_probs * (grad_probs - row_terms)).astype(jnp.bfloat16)
    grad_query = jnp.einsum(
        "ghqk,gkhd->gqhd", grad_scores, key_block, preferred_element_type=jnp.float32
    ) * HEAD_DIM ** (-0.5)
    grad_key = jnp.einsum(
        "ghqk,gqhd->gkhd", grad_scores, query_block, preferred_element_type=jnp.float32
    ) * HEAD_DIM ** (-0.5)
    grad_value = jnp.einsum(
        "ghqk,gqhd->gkhd",
        attn_probs.astype(jnp.bfloat16),
        grad_att,
        preferred_element_type=jnp.float32,
    )
    return jnp.stack([grad_query, grad_key, grad_value], axis=2)


def run_block(flat_rows, modulation, weights, images, length):
    full_qkv, full_proj, full_fc1, full_fc2, bias_qv, bias_proj, bias_fc1, bias_fc2 = weights
    width = flat_rows.shape[1]
    heads = width // HEAD_DIM
    pieces = jnp.split(modulation, 6)
    h_first = modulate(flat_rows, pieces[0], pieces[1]).astype(jnp.bfloat16)
    qkv_bias = jnp.concatenate(
        [bias_qv[:width], jnp.zeros((width,), jnp.bfloat16), bias_qv[width:]]
    ).astype(jnp.float32)
    qkv_rows = (jnp.dot(h_first, full_qkv, preferred_element_type=jnp.float32) + qkv_bias).astype(
        jnp.bfloat16
    )
    split_rows = qkv_rows.reshape(images // 2, 2, length, 3, heads, HEAD_DIM)
    attended, log_total = lax.map(
        attend_pair, (split_rows[:, :, :, 0], split_rows[:, :, :, 1], split_rows[:, :, :, 2])
    )
    attended = attended.reshape(images * length, width).astype(jnp.bfloat16)
    branch = jnp.dot(attended, full_proj, preferred_element_type=jnp.float32) + bias_proj.astype(
        jnp.float32
    )
    middle = flat_rows + pieces[2] * branch
    h_second = modulate(middle, pieces[3], pieces[4]).astype(jnp.bfloat16)
    pre_act = jnp.dot(h_second, full_fc1, preferred_element_type=jnp.float32) + bias_fc1.astype(
        jnp.float32
    )
    hidden = gelu_tanh(pre_act).astype(jnp.bfloat16)
    mlp_out = jnp.dot(hidden, full_fc2, preferred_element_type=jnp.float32) + bias_fc2.astype(
        jnp.float32
    )
    result = middle + pieces[5] * mlp_out
    return (
        h_first,
        split_rows,
        log_total,
        attended,
        branch,
        middle,
        h_second,
        pre_act,
        hidden,
        mlp_out,
        result,
    )


def on_device(
    latents,
    cond,
    live,
    w_ada,
    b_ada,
    w_qkv,
    b_qv,
    w_proj,
    b_proj,
    w_fc1,
    b_fc1,
    w_fc2,
    b_fc2,
    cotangent,
):
    images = latents.shape[1]
    length = latents.shape[2]
    width = latents.shape[3]
    heads = width // HEAD_DIM
    scaled = jax.nn.silu(cond[0]).astype(jnp.bfloat16)
    mod_part = jnp.dot(scaled, w_ada, preferred_element_type=jnp.float32) + b_ada.astype(
        jnp.float32
    )
    modulation = lax.all_gather(mod_part, "fsdp", axis=0, tiled=True)
    gathered = (
        lax.all_gather(w_qkv, "fsdp", axis=0, tiled=True),
        lax.all_gather(w_proj, "fsdp", axis=0, tiled=True),
        lax.all_gather(w_fc1, "fsdp", axis=0, tiled=True),
        lax.all_gather(w_fc2, "fsdp", axis=0, tiled=True),
        lax.all_gather(b_qv, "fsdp", axis=0, tiled=True),
        lax.all_gather(b_proj, "fsdp", axis=0, tiled=True),
        lax.all_gather(b_fc1, "fsdp", axis=0, tiled=True),
        lax.all_gather(b_fc2, "fsdp", axis=0, tiled=True),
    )
    flat_rows = latents[0].reshape(images * length, width).astype(jnp.float32)
    live_mask = (lax.iota(jnp.int32, images) < live[0, 0]).astype(jnp.float32)
    row_mask = jnp.repeat(live_mask, length)[:, None]
    forward_run = run_block(flat_rows, modulation, gathered, images, length)
    block_out = (forward_run[10] * row_mask).astype(jnp.bfloat16).reshape(latents.shape)
    weights = (
        lax.all_gather(w_qkv, "fsdp", axis=0, tiled=True),
        lax.all_gather(w_proj, "fsdp", axis=0, tiled=True),
        lax.all_gather(w_fc1, "fsdp", axis=0, tiled=True),
        lax.all_gather(w_fc2, "fsdp", axis=0, tiled=True),
        lax.all_gather(b_qv, "fsdp", axis=0, tiled=True),
        lax.all_gather(b_proj, "fsdp", axis=0, tiled=True),
        lax.all_gather(b_fc1, "fsdp", axis=0, tiled=True),
        lax.all_gather(b_fc2, "fsdp", axis=0, tiled=True),
    )
    full_qkv, full_proj, full_fc1, full_fc2 = (weights[0], weights[1], weights[2], weights[3])
    saved = run_block(flat_rows, modulation, weights, images, length)
    (
        h_first,
        split_rows,
        log_total,
        attended,
        branch,
        middle,
        h_second,
        pre_act,
        hidden,
        mlp_out,
        result,
    ) = saved
    pieces = jnp.split(modulation, 6)
    grad_res = cotangent[0].reshape(images * length, width).astype(jnp.float32) * row_mask
    grad_out = (pieces[5] * grad_res).astype(jnp.bfloat16)
    grad_gate_two = jnp.sum(grad_res * mlp_out, axis=0)
    grad_fc2 = jnp.einsum("rf,rd->fd", hidden, grad_out, preferred_element_type=jnp.float32)
    grad_bfc2 = jnp.sum(grad_out.astype(jnp.float32), axis=0)
    grad_hidden = jnp.einsum("rd,fd->rf", grad_out, full_fc2, preferred_element_type=jnp.float32)
    gelu_pull = jax.vjp(gelu_tanh, pre_act)[1]
    grad_pre = gelu_pull(grad_hidden)[0].astype(jnp.bfloat16)
    grad_fc1 = jnp.einsum("rd,rf->df", h_second, grad_pre, preferred_element_type=jnp.float32)
    grad_bfc1 = jnp.sum(grad_pre.astype(jnp.float32), axis=0)
    grad_h2 = jnp.einsum("rf,df->rd", grad_pre, full_fc1, preferred_element_type=jnp.float32)
    second_pull = jax.vjp(modulate, middle, pieces[3], pieces[4])[1]
    grad_mid_norm, grad_shift_two, grad_scale_two = second_pull(grad_h2)
    grad_mid = grad_res + grad_mid_norm
    grad_branch = (pieces[2] * grad_mid).astype(jnp.bfloat16)
    grad_gate_one = jnp.sum(grad_mid * branch, axis=0)
    grad_proj = jnp.einsum("rd,re->de", attended, grad_branch, preferred_element_type=jnp.float32)
    grad_bproj = jnp.sum(grad_branch.astype(jnp.float32), axis=0)
    grad_att = jnp.einsum(
        "re,de->rd", grad_branch, full_proj, preferred_element_type=jnp.float32
    ).astype(jnp.bfloat16)
    grad_att = grad_att.reshape(images // 2, 2, length, heads, HEAD_DIM)
    grad_qkv = lax.map(
        attend_back,
        (
            split_rows[:, :, :, 0],
            split_rows[:, :, :, 1],
            split_rows[:, :, :, 2],
            log_total,
            grad_att,
        ),
    )
    grad_qkv = grad_qkv.reshape(images * length, 3 * width).astype(jnp.bfloat16)
    grad_wqkv = jnp.einsum("rd,re->de", h_first, grad_qkv, preferred_element_type=jnp.float32)
    qkv_sums = jnp.sum(grad_qkv.astype(jnp.float32), axis=0)
    grad_bqv = jnp.concatenate([qkv_sums[:width], qkv_sums[2 * width :]])
    grad_h1 = jnp.einsum("re,de->rd", grad_qkv, full_qkv, preferred_element_type=jnp.float32)
    first_pull = jax.vjp(modulate, flat_rows, pieces[0], pieces[1])[1]
    grad_rows_norm, grad_shift_one, grad_scale_one = first_pull(grad_h1)
    grad_rows = grad_mid + grad_rows_norm
    grad_mod = jnp.concatenate(
        [
            grad_shift_one,
            grad_scale_one,
            grad_gate_one,
            grad_shift_two,
            grad_scale_two,
            grad_gate_two,
        ]
    )
    shards = (
        lax.psum_scatter(grad_wqkv, "fsdp", scatter_dimension=0, tiled=True),
        lax.psum_scatter(grad_proj, "fsdp", scatter_dimension=0, tiled=True),
        lax.psum_scatter(grad_fc1, "fsdp", scatter_dimension=0, tiled=True),
        lax.psum_scatter(grad_fc2, "fsdp", scatter_dimension=0, tiled=True),
        lax.psum_scatter(grad_bqv, "fsdp", scatter_dimension=0, tiled=True),
        lax.psum_scatter(grad_bproj, "fsdp", scatter_dimension=0, tiled=True),
        lax.psum_scatter(grad_bfc1, "fsdp", scatter_dimension=0, tiled=True),
        lax.psum_scatter(grad_bfc2, "fsdp", scatter_dimension=0, tiled=True),
        lax.psum_scatter(grad_mod, "fsdp", scatter_dimension=0, tiled=True),
    )
    mod_mine = shards[8]
    grad_wada = scaled.astype(jnp.float32)[:, None] * mod_mine[None, :]
    grad_scaled = jnp.dot(w_ada.astype(jnp.float32), mod_mine, precision=lax.Precision.HIGHEST)
    grad_scaled = lax.psum(grad_scaled, "fsdp")
    silu_pull = jax.vjp(jax.nn.silu, cond[0])[1]
    grad_cond = silu_pull(grad_scaled)[0][None, :]
    totals = lax.psum(
        (
            shards[0],
            shards[1],
            shards[2],
            shards[3],
            shards[4],
            shards[5],
            shards[6],
            shards[7],
            grad_wada,
            mod_mine,
        ),
        "bin",
    )
    return (
        block_out,
        grad_rows.reshape(latents.shape),
        grad_cond,
        totals[8],
        totals[9],
        totals[0],
        totals[4],
        totals[1],
        totals[5],
        totals[2],
        totals[6],
        totals[3],
        totals[7],
    )


def solution(mesh):
    return jax.shard_map(
        on_device,
        mesh=mesh,
        in_specs=(
            P("bin", "fsdp", None, None),
            P("bin", None),
            P("bin", "fsdp"),
            P(None, "fsdp"),
            P("fsdp"),
            P("fsdp", None),
            P("fsdp"),
            P("fsdp", None),
            P("fsdp"),
            P("fsdp", None),
            P("fsdp"),
            P("fsdp", None),
            P("fsdp"),
            P("bin", "fsdp", None, None),
        ),
        out_specs=(
            P("bin", "fsdp", None, None),
            P("bin", "fsdp", None, None),
            P("bin", None),
            P(None, "fsdp"),
            P("fsdp"),
            P("fsdp", None),
            P("fsdp"),
            P("fsdp", None),
            P("fsdp"),
            P("fsdp", None),
            P("fsdp"),
            P("fsdp", None),
            P("fsdp"),
        ),
        check_vma=False,
    )
```

profile of v0, /device:TPU:0, one launch (start us, length us, event | category | flops | bytes accessed | tf_op | source)
XLA Modules:
  0.0 1843.6 jit_solution(338678586922015093)
XLA Ops:
  16.1 40.7 %all-reduce.13 = (bf16[2304]{0:T(1024)(128)(2,1)S(1)}, bf16[1152]{0:T(1024)(128)(2,1)S(1)}, bf16[1152]{0:T(1024)(128)(2,1)}, bf16[4608]{0:T(1024)(128)(2,1)S(1)}) all-reduce(bf16[2304]{0:T(1024)(128)(2,1)S(1)} %dynamic-update-slice.1, bf16[1152]{0:T(1024)(128)(2,1)S(1)} %dynamic-update-slice.2, ...), channel_id=1, replica_groups=mesh['bin'=4,'fsdp'=8] {'fsdp'}, use_global_device_ids=true, to_apply=%add.1 | all-reduce | flops 9216 | bytes 36864
  58.9 34.5 %all-reduce = f32[6912]{0:T(1024)S(1)} all-reduce(f32[6912]{0:T(1024)S(1)} %add_dynamic-update-slice_fusion), channel_id=1, replica_groups=mesh['bin'=4,'fsdp'=8] {'fsdp'}, use_global_device_ids=true, to_apply=%add | all-reduce | flops 6912 | bytes 55296
  93.5 2.6 multiply_convert_fusion.4
  96.2 1.5 fusion.21
  97.7 36.3 %all-gather.5.cloned.1.call-done = bf16[1152,3456]{1,0:T(8,128)(2,1)} async-done(((bf16[144,3456]{1,0:T(8,128)(2,1)}), bf16[1152,3456]{1,0:T(8,128)(2,1)}) %all-gather.5.cloned.1.call-update) | async-done | bytes 7962640 | tf_op jit(solution)/shard_map/all_gather | solution.py:140
  134.0 10.3 add_convert_fusion
  144.3 13.6 reshape.274
  157.9 6.0 fusion.57
  163.9 4.1 copy.72
  168.0 4.1 copy.71
  172.2 4.1 copy.70
  176.3 2.9 multiply_reduce_fusion.1
  179.3 1.6 fusion.6
  180.9 1.7 copy-done.1
  182.6 14.0 fusion.32
  199.1 6.0 fusion.56
  205.1 1.4 copy-done.3
  206.9 135.9 %all-gather.9.cloned.1.call-done = bf16[1152,4608]{1,0:T(8,128)(2,1)} async-done(((bf16[144,4608]{1,0:T(8,128)(2,1)}), bf16[1152,4608]{1,0:T(8,128)(2,1)}) %all-gather.9.cloned.1.call-update) | async-done | bytes 10616848 | tf_op jit(solution)/shard_map/all_gather | solution.py:142
  342.8 12.2 fusion.51
  355.0 140.5 %all-gather.11.cloned.1.call-done = bf16[4608,1152]{1,0:T(8,128)(2,1)} async-done(((bf16[576,1152]{1,0:T(8,128)(2,1)}), bf16[4608,1152]{1,0:T(8,128)(2,1)}) %all-gather.11.cloned.1.call-update) | async-done | bytes 10616848 | tf_op jit(solution)/shard_map/all_gather | solution.py:143
  495.5 18.9 %convert_reduce_fusion = (f32[4608]{0:T(1024)S(1)}, bf16[512,4608]{1,0:T(8,128)(2,1)}) fusion(f32[512,4608]{1,0:T(8,128)} %fusion.51, f32[4608]{0:T(1024)S(1)} %convert_element_type.166, bf16[512,1152]{1,0:T(8,128)(2,1)} %multiply_convert_fusion.4, bf16[4608,1152]{1,0:T(8,128)(2,1)} %all-gather.11.cloned.1.call-done), kind=kOutput, calls=%fused_computation.10 | convolution fusion | flops 5499514368 | bytes 25989120 | tf_op jit(solution)/shard_map/rd,fd->rf/dot_general | solution.py:185
  514.3 11.6 multiply_reduce_fusion.3
  529.1 4.0 fusion.63
  533.6 1.6 fusion.26
  535.2 4.7 convolution_convert_fusion
  539.9 5.7 reshape.275
  545.6 4.1 copy.56
  549.7 6.6 multiply_reduce_fusion
  556.4 4.8 multiply_convert_fusion.1
  563.9 1.6 fusion.28
  566.7 3.6 copy.61
  571.2 1.8 copy-done.16
  572.9 7.9 fusion.62
  580.9 13.0 fusion.50
  594.0 14.8 fusion.52
  610.2 9.9 fusion.27
  622.2 15.5 multiply_reduce_fusion.2
  637.8 35.9 %all-reduce.5 = f32[6912]{0:T(1024)S(1)} all-reduce(f32[6912]{0:T(1024)S(1)} %constant_dynamic-update-slice_fusion), channel_id=2, replica_groups=mesh['bin'=4,'fsdp'=8] {'fsdp'}, use_global_device_ids=true, to_apply=%region_17.18.clone | all-reduce | flops 6912 | bytes 55296
  673.8 2.3 broadcast_multiply_fusion
  676.0 232.5 %reduce-scatter.5.cloned.1.call-done = f32[144,3456]{1,0:T(8,128)} async-done(((f32[1152,3456]{1,0:T(8,128)}), f32[144,3456]{1,0:T(8,128)}) %reduce-scatter.5.cloned.1.call-update) | async-done | bytes 1990672 | tf_op jit(solution)/shard_map/reduce_scatter | solution.py:231
  908.6 350.7 %reduce-scatter.9.cloned.1.call-done = f32[144,4608]{1,0:T(8,128)} async-done(((f32[1152,4608]{1,0:T(8,128)}), f32[144,4608]{1,0:T(8,128)}) %reduce-scatter.9.cloned.1.call-update) | async-done | bytes 2654224 | tf_op jit(solution)/shard_map/reduce_scatter | solution.py:233
  1259.3 350.3 %reduce-scatter.11.cloned.1.call-done = f32[576,1152]{1,0:T(8,128)} async-done(((f32[4608,1152]{1,0:T(8,128)}), f32[576,1152]{1,0:T(8,128)}) %reduce-scatter.11.cloned.1.call-update) | async-done | bytes 2654224 | tf_op jit(solution)/shard_map/reduce_scatter | solution.py:234
  1613.2 35.7 %all-reduce.10 = (f32[1152]{0:T(1024)S(1)}, f32[2304]{0:T(1024)S(1)}, f32[1152]{0:T(1024)S(1)}, f32[4608]{0:T(1024)S(1)}, f32[1152]{0:T(1024)S(1)}) all-reduce(f32[1152]{0:T(1024)S(1)} %convolution_reduce_fusion, f32[2304]{0:T(1024)S(1)} %pad_maximum_fusion, ...), channel_id=1, replica_groups=mesh['bin'=4,'fsdp'=8] {'fsdp'}, use_global_device_ids=true, to_apply=%region_18.19 | all-reduce | flops 10368 | bytes 82944 | tf_op jit(solution)/shard_map/psum | solution.py:244
  1649.9 12.5 all-reduce.11
  1662.4 162.9 %all-reduce.16.cloned.1.call-done = (f32[1152,864]{0,1:T(8,128)}, f32[144,3456]{1,0:T(8,128)}, f32[144,1152]{1,0:T(8,128)}, f32[144,4608]{1,0:T(8,128)}, f32[576,1152]{1,0:T(8,128)}) async-done(((f32[1152,864]{0,1:T(8,128)}, f32[144,3456]{1,0:T(8,128)}, f32[144,1152]{1,0:T(8,128)}, f32[144,4608]{1,0:T(8,128)}, f32[576,1152]{1,0:T(8,128)}), (f32[1152,864]{0,1:T(8,128)}, f32[144,3456]{1,0:T(8,128)}, ...) | async-done | bytes 11943952 | tf_op jit(solution)/shard_map/psum | solution.py:247
  1825.2 4.5 copy.95
  1832.6 1.5 copy.98
  1835.3 1.5 copy.99
  (186 shorter events, 28.2 us)
Async XLA Ops:
  7.2 51.0 %copy-start = (bf16[1152,864]{0,1:T(8,128)(2,1)S(1)}, bf16[1152,864]{0,1:T(8,128)(2,1)}, u32[]{:S(2)}) copy-start(bf16[1152,864]{0,1:T(8,128)(2,1)} %param.17) | copy-start | bytes 5971972
  7.2 4.7 copy-start.40
  7.2 4.1 copy-start.36
  7.2 7.9 copy-start.44
  7.2 8.2 copy-start.45
  7.2 8.4 copy-start.43
  7.2 8.7 copy-start.41
  7.3 49.6 %copy-start.2 = (bf16[1,2,256,1152]{3,2,1,0:T(8,128)(2,1)S(1)}, bf16[1,2,256,1152]{3,2,1,0:T(8,128)(2,1)}, u32[]{:S(2)}) copy-start(bf16[1,2,256,1152]{3,2,1,0:T(8,128)(2,1)} %param.14) | copy-start | bytes 3538948
  7.3 126.8 %all-gather.5.cloned.1.call-start = ((), (), s32[]{:S(2)}) async-start(), calls=%async_computation.4 | async-start | bytes 8957952 | tf_op jit(solution)/shard_map/all_gather | solution.py:140
  8.0 191.1 %all-gather.7.cloned.1.call-start = ((), (), s32[]{:S(2)}) async-start(), calls=%async_computation.5 | async-start | bytes 2985984 | tf_op jit(solution)/shard_map/all_gather | solution.py:141
  8.8 334.0 %all-gather.9.cloned.1.call-start = ((), (), s32[]{:S(2)}) async-start(), calls=%async_computation.6 | async-start | bytes 11943936 | tf_op jit(solution)/shard_map/all_gather | solution.py:142
  9.5 486.0 %all-gather.11.cloned.1.call-start = ((), (), s32[]{:S(2)}) async-start(), calls=%async_computation.7 | async-start | bytes 11943936 | tf_op jit(solution)/shard_map/all_gather | solution.py:143
  10.1 48.7 %copy-start.42 = (bf16[864]{0:T(1024)(128)(2,1)S(1)}, bf16[864]{0:T(1024)(128)(2,1)}, u32[]{:S(2)}) copy-start(bf16[864]{0:T(1024)(128)(2,1)} %param.18) | copy-start | bytes 5188
  10.1 666.0 %reduce-scatter.7.cloned.1.call-start = ((), (), s32[]{:S(2)}) async-start(), calls=%async_computation.9 | async-start | bytes 5971968 | tf_op jit(solution)/shard_map/reduce_scatter | solution.py:232
  11.3 82.2 %copy-start.27 = (f32[1152]{0:T(1024)}, f32[1152]{0:T(1024)S(1)}, u32[]{:S(2)}) copy-start(f32[1152]{0:T(1024)S(1)} %reduce.4) | copy-start | bytes 13828
  58.1 39.6 %copy-start.30 = (f32[512]{0:T(512)}, f32[512]{0:T(512)S(1)}, u32[]{:S(2)}) copy-start(f32[512]{0:T(512)S(1)} %rsqrt.27) | copy-start | bytes 6148
  58.1 39.6 %copy-start.32 = (f32[1,2,2,128]{3,1,2,0:T(2,128)}, f32[1,2,2,128]{3,1,2,0:T(2,128)S(1)}, u32[]{:S(2)}) copy-start(f32[1,2,2,128]{3,1,2,0:T(2,128)S(1)} %copy.73) | copy-start | bytes 6148
  93.5 4.2 copy-start.25
  179.3 3.3 copy-start.1
  179.3 3.3 copy-start.14
  495.5 18.9 %copy-start.4 = (f32[512,1152]{1,0:T(8,128)S(1)}, f32[512,1152]{1,0:T(8,128)}, u32[]{:S(2)}) copy-start(f32[512,1152]{1,0:T(8,128)} %copy-done.3) | copy-start | bytes 7077892
  526.7 1.4 copy-start.12
  527.2 1.9 copy-start.15
  533.2 375.4 %reduce-scatter.5.cloned.1.call-start = ((), (), s32[]{:S(2)}) async-start(), calls=%async_computation.8 | async-start | bytes 17915904 | tf_op jit(solution)/shard_map/reduce_scatter | solution.py:231
  533.6 1.6 copy-start.23
  549.7 13.8 slice-start
  556.4 4.9 copy-start.8
  556.4 7.1 slice-start.1
  570.4 2.5 copy-start.21
  571.1 1.8 copy-start.16
  580.9 678.4 %reduce-scatter.9.cloned.1.call-start = ((), (), s32[]{:S(2)}) async-start(), calls=%async_computation.10 | async-start | bytes 23887872 | tf_op jit(solution)/shard_map/reduce_scatter | solution.py:233
  594.0 1015.7 %reduce-scatter.11.cloned.1.call-start = ((), (), s32[]{:S(2)}) async-start(), calls=%async_computation.11 | async-start | bytes 23887872 | tf_op jit(solution)/shard_map/reduce_scatter | solution.py:234
  608.9 1216.4 %all-reduce.16.cloned.1.call-start = ((), (), s32[]{:S(2)}) async-start(), calls=%async_computation.12 | async-start | bytes 23887872 | tf_op jit(solution)/shard_map/psum | solution.py:247
  610.2 10.0 copy-start.35
  610.2 10.0 copy-start.31
  610.2 11.2 copy-start.13
  610.2 11.2 copy-start.19
  620.2 1.7 copy-start.5
  620.2 2.0 copy-start.10
  620.2 2.0 copy-start.26
  622.2 51.6 %copy-start.29 = (f32[1152]{0:T(1024)S(1)}, f32[1152]{0:T(1024)}, u32[]{:S(2)}) copy-start(f32[1152]{0:T(1024)} %get-tuple-element.94) | copy-start | bytes 13828
  1609.6 2.1 copy-start.11
  1609.6 2.1 copy-start.39
  1609.7 39.3 %copy-start.28 = (f32[1152]{0:T(1024)S(1)}, f32[1152]{0:T(1024)}, u32[]{:S(2)}) copy-start(f32[1152]{0:T(1024)} %copy-done.27) | copy-start | bytes 13828
  1825.2 4.5 copy-start.20
  1829.7 1.5 copy-start.24
  1829.7 2.9 copy-start.18
  1832.6 2.7 copy-start.17
  (9 other events, 9.5 us)
Sparse Core Ops, SparseCore 0:
  10.3 123.7 all-gather.4
  136.2 53.2 all-gather.6
  191.7 151.0 all-gather.8
  344.8 150.6 all-gather.10
  533.3 102.3 reduce-scatter.6
  639.9 268.5 reduce-scatter.4
  912.9 346.3 reduce-scatter.8
  1263.2 346.4 reduce-scatter.10
  1613.5 211.7 all-reduce.15
where the time goes:
time: 1850 us; the launch traced here: 1840 us
  waiting for transfers between devices  1410 us (76%)
  blocking collectives  159 us (9%)
  matrix products  158 us (9%)
  local copies, waits for them, and re-layouts  72.8 us (4%)
  between operations  20.8 us (1%)
  other arithmetic  20.4 us (1%)
    reduce_scatter x1, waiting for transfers between devices, on_device(): lax.psum_scatter(grad_fc1, 'fsdp', scatter_dimension=0, tiled=True)  351 us
    reduce_scatter x1, waiting for transfers between devices, on_device(): lax.psum_scatter(grad_fc2, 'fsdp', scatter_dimension=0, tiled=True)  350 us
    reduce_scatter x1, waiting for transfers between devices, on_device(): lax.psum_scatter(grad_wqkv, 'fsdp', scatter_dimension=0, tiled=True)  233 us
    psum x1, waiting for transfers between devices, on_device(): lax.psum((shards[0], shards[1], shards[2], shards[3], shards[4], shards[5...  163 us
    all_gather x1, waiting for transfers between devices, on_device(): lax.all_gather(w_fc2, 'fsdp', axis=0, tiled=True)  140 us
    all_gather x1, waiting for transfers between devices, on_device(): lax.all_gather(w_fc1, 'fsdp', axis=0, tiled=True)  136 us
    unnamed x3, blocking collectives  111 us
    unnamed x128, local copies, waits for them, and re-layouts  37.7 us
  transfers between devices with their start and end apart: 9, of which 7 were waited for; matrix products, arithmetic and copies ran while one was open for 11% of the time, Pallas kernels for 0%

commit v1 on v0

--- a/solution.py
+++ b/solution.py
@@ -4,6 +4,28 @@
 from jax.sharding import PartitionSpec as P
 
 HEAD_DIM = 72
+
+
+def shape_ranges(frame, which_dim):
+    local_now = list(frame.shape[1:])
+    local_now[which_dim] *= frame.shape[0]
+    base_arr = jnp.moveaxis(frame, 0, which_dim).reshape(local_now)
+    return base_arr
+
+
+def balance_the_strips_all(inp, comm_axis):
+    r2 = inp[None]
+    k_all = lax.axis_size(comm_axis)
+    for b in range(k_all.bit_length() - 1):
+        fresh = 1 << b
+        field_out = lax.ppermute(
+            r2, axis_name=comm_axis, perm=[(d, d ^ fresh) for d in range(k_all)]
+        )
+        now = jnp.stack([r2, field_out])
+        h_now = lax.axis_index(comm_axis)
+        z2 = h_now >> b & 1
+        r2 = jnp.where(z2 == 0, now, now[::-1]).reshape(-1, *inp.shape)
+    return r2
 
 
 def layer_norm(field):
@@ -136,11 +158,17 @@
         jnp.float32
     )
     modulation = lax.all_gather(mod_part, "fsdp", axis=0, tiled=True)
+
+    def _close_entries(local, x_local, where_dim=0):
+        moved = balance_the_strips_all(local, x_local)
+        taken_in = shape_ranges(moved, where_dim)
+        return taken_in
+
     gathered = (
         lax.all_gather(w_qkv, "fsdp", axis=0, tiled=True),
         lax.all_gather(w_proj, "fsdp", axis=0, tiled=True),
         lax.all_gather(w_fc1, "fsdp", axis=0, tiled=True),
-        lax.all_gather(w_fc2, "fsdp", axis=0, tiled=True),
+        _close_entries(w_fc2, "fsdp"),
         lax.all_gather(b_qv, "fsdp", axis=0, tiled=True),
         lax.all_gather(b_proj, "fsdp", axis=0, tiled=True),
         lax.all_gather(b_fc1, "fsdp", axis=0, tiled=True),

time: 1850 us -> 2070 us (1.12)
  blocking collectives: 159 us -> 456 us
  waiting for transfers between devices: 1410 us -> 1310 us
  other arithmetic: 20.4 us -> 47.9 us
    unnamed x3, blocking collectives: 111 us -> 408 us
    reduce_scatter x1, waiting for transfers between devices: 233 us -> 0.01 us  [on_device(): lax.psum_scatter(grad_wqkv, 'fsdp', scatter_dimension=0, tiled=True)]
    ppermute x0 -> x3, waiting for transfers between devices: none -> 176 us  [balance_the_strips_all(): lax.ppermute(r2, axis_name=comm_axis, perm=[(d, d ^ fresh) for d in range...]
    reduce_scatter x1, waiting for transfers between devices: 351 us -> 324 us  [on_device(): lax.psum_scatter(grad_fc1, 'fsdp', scatter_dimension=0, tiled=True)]
    psum x1, waiting for transfers between devices: 163 us -> 138 us  [on_device(): lax.psum((shards[0], shards[1], shards[2], shards[3], shards[4], shards[5...]
  transfers between devices with their start and end apart: 9 -> 12, of which waited for: 7 -> 9; matrix products, arithmetic and copies ran while one was open for 11% -> 10% of each run, Pallas kernels for 0% -> 0%
where the time goes in v1:
time: 2070 us; the launch traced here: 2060 us
  waiting for transfers between devices  1310 us (63%)
  blocking collectives  456 us (22%)
  matrix products  150 us (7%)
  local copies, waits for them, and re-layouts  73.3 us (4%)
  other arithmetic  47.9 us (2%)
  between operations  21 us (1%)
    unnamed x3, blocking collectives  408 us
    reduce_scatter x1, waiting for transfers between devices, on_device(): lax.psum_scatter(grad_fc2, 'fsdp', scatter_dimension=0, tiled=True)  350 us
    reduce_scatter x1, waiting for transfers between devices, on_device(): lax.psum_scatter(grad_fc1, 'fsdp', scatter_dimension=0, tiled=True)  324 us
    ppermute x3, waiting for transfers between devices, balance_the_strips_all(): lax.ppermute(r2, axis_name=comm_axis, perm=[(d, d ^ fresh) for d in range...  176 us
    all_gather x1, waiting for transfers between devices, on_device(): lax.all_gather(w_fc1, 'fsdp', axis=0, tiled=True)  146 us
    all_gather x1, waiting for transfers between devices, on_device(): lax.all_gather(w_fc2, 'fsdp', axis=0, tiled=True)  138 us
    psum x1, waiting for transfers between devices, on_device(): lax.psum((shards[0], shards[1], shards[2], shards[3], shards[4], shards[5...  138 us
  transfers between devices with their start and end apart: 12, of which 9 were waited for; matrix products, arithmetic and copies ran while one was open for 10% of the time, Pallas kernels for 0%

profile of v1, /device:TPU:0, one launch (start us, length us, event | category | flops | bytes accessed | tf_op | source)
XLA Modules:
  0.0 2064.4 jit_solution(2047326041665647117)
XLA Ops:
  15.8 40.8 %all-reduce.13 = (bf16[2304]{0:T(1024)(128)(2,1)S(1)}, bf16[1152]{0:T(1024)(128)(2,1)S(1)}, bf16[4608]{0:T(1024)(128)(2,1)S(1)}, bf16[1152]{0:T(1024)(128)(2,1)}) all-reduce(bf16[2304]{0:T(1024)(128)(2,1)S(1)} %dynamic-update-slice.1, bf16[1152]{0:T(1024)(128)(2,1)S(1)} %dynamic-update-slice.2, ...), channel_id=1, replica_groups=mesh['bin'=4,'fsdp'=8] {'fsdp'}, use_global_device_ids=true, to_apply=%add.1 | all-reduce | flops 9216 | bytes 36864
  58.1 34.7 %all-reduce = f32[6912]{0:T(1024)S(1)} all-reduce(f32[6912]{0:T(1024)S(1)} %add_dynamic-update-slice_fusion), channel_id=1, replica_groups=mesh['bin'=4,'fsdp'=8] {'fsdp'}, use_global_device_ids=true, to_apply=%add | all-reduce | flops 6912 | bytes 55296
  96.0 38.0 %all-gather.5.cloned.1.call-done = bf16[1152,3456]{1,0:T(8,128)(2,1)} async-done(((bf16[144,3456]{1,0:T(8,128)(2,1)}), bf16[1152,3456]{1,0:T(8,128)(2,1)}) %all-gather.5.cloned.1.call-update) | async-done | bytes 7962640 | tf_op jit(solution)/shard_map/all_gather | solution.py:168
  134.0 10.3 add_convert_fusion
  144.3 13.6 reshape.282
  157.9 6.0 fusion.65
  163.9 4.1 copy.71
  168.0 4.1 copy.72
  172.1 4.1 copy.70
  176.3 2.9 multiply_reduce_fusion.1
  182.6 2.2 fusion.40
  187.3 2.2 all-gather.7.cloned.1.call-done
  189.5 5.6 fusion.64
  196.9 145.9 %all-gather.9.cloned.1.call-done = bf16[1152,4608]{1,0:T(8,128)(2,1)} async-done(((bf16[144,4608]{1,0:T(8,128)(2,1)}), bf16[1152,4608]{1,0:T(8,128)(2,1)}) %all-gather.9.cloned.1.call-update) | async-done | bytes 10616848 | tf_op jit(solution)/shard_map/all_gather | solution.py:170
  342.8 14.4 multiply_convert_fusion
  357.2 138.3 %all-gather.11.cloned.1.call-done = bf16[4608,1152]{1,0:T(8,128)(2,1)} async-done(((bf16[576,1152]{1,0:T(8,128)(2,1)}), bf16[4608,1152]{1,0:T(8,128)(2,1)}) %all-gather.11.cloned.1.call-update) | async-done | bytes 10616848 | tf_op jit(solution)/shard_map/all_gather | solution.py:186
  495.5 18.0 convert_reduce_fusion
  513.5 12.3 multiply_reduce_fusion.2
  530.4 4.2 fusion.71
  536.2 4.7 convolution_convert_fusion
  540.9 6.1 reshape.283
  546.9 4.1 copy.56
  551.1 6.7 multiply_reduce_fusion
  557.7 4.9 multiply_convert_fusion.1
  568.1 3.6 copy.61
  574.3 7.9 fusion.70
  582.3 13.1 fusion.60
  595.5 12.9 fusion.49
  609.3 37.4 %collective-permute-done = bf16[1,576,1152]{2,1,0:T(8,128)(2,1)} collective-permute-done((bf16[1,576,1152]{2,1,0:T(8,128)(2,1)}, bf16[1,576,1152]{2,1,0:T(8,128)(2,1)}, u32[]{:S(2)}, u32[]{:S(2)}) %collective-permute-start) | collective-permute-done | bytes 1327136 | tf_op jit(solution)/shard_map/ppermute | solution.py:21
  646.8 2.0 pad_maximum_fusion.2
  648.8 2.9 fusion.34
  651.7 138.7 %collective-permute-done.1 = bf16[2,576,1152]{2,1,0:T(8,128)(2,1)} collective-permute-done((bf16[2,576,1152]{2,1,0:T(8,128)(2,1)}, bf16[2,576,1152]{2,1,0:T(8,128)(2,1)}, u32[]{:S(2)}, u32[]{:S(2)}) %collective-permute-start.1) | collective-permute-done | bytes 2654240 | tf_op jit(solution)/shard_map/ppermute | solution.py:21
  790.4 3.2 pad_maximum_fusion.1
  793.5 3.3 reverse_select_fusion.1
  801.7 10.4 fusion.32
  814.7 6.5 fusion.39
  821.2 332.9 %all-reduce.5 = f32[6912]{0:T(1024)S(1)} all-reduce(f32[6912]{0:T(1024)S(1)} %constant_dynamic-update-slice_fusion), channel_id=2, replica_groups=mesh['bin'=4,'fsdp'=8] {'fsdp'}, use_global_device_ids=true, to_apply=%region_17.18.clone | all-reduce | flops 6912 | bytes 55296
  1154.2 2.3 broadcast_multiply_fusion
  1156.4 324.1 %reduce-scatter.9.cloned.1.call-done = f32[144,4608]{1,0:T(8,128)} async-done(((f32[1152,4608]{1,0:T(8,128)}), f32[144,4608]{1,0:T(8,128)}) %reduce-scatter.9.cloned.1.call-update) | async-done | bytes 2654224 | tf_op jit(solution)/shard_map/reduce_scatter | solution.py:261
  1480.5 349.7 %reduce-scatter.11.cloned.1.call-done = f32[576,1152]{1,0:T(8,128)} async-done(((f32[4608,1152]{1,0:T(8,128)}), f32[576,1152]{1,0:T(8,128)}) %reduce-scatter.11.cloned.1.call-update) | async-done | bytes 2654224 | tf_op jit(solution)/shard_map/reduce_scatter | solution.py:262
  1830.3 5.7 pad_maximum_fusion
  1836.0 5.4 reverse_select_fusion
  1842.5 35.7 %all-reduce.10 = (f32[1152]{0:T(1024)S(1)}, f32[2304]{0:T(1024)S(1)}, f32[1152]{0:T(1024)S(1)}, f32[4608]{0:T(1024)S(1)}, f32[1152]{0:T(1024)S(1)}) all-reduce(f32[1152]{0:T(1024)S(1)} %convolution_reduce_fusion, f32[2304]{0:T(1024)S(1)} %pad_maximum_fusion.3, ...), channel_id=1, replica_groups=mesh['bin'=4,'fsdp'=8] {'fsdp'}, use_global_device_ids=true, to_apply=%region_18.19 | all-reduce | flops 10368 | bytes 82944 | tf_op jit(solution)/shard_map/psum | solution.py:272
  1879.1 12.3 all-reduce.11
  1891.4 4.5 add_add_fusion.2
  1895.8 12.2 fusion.17
  1908.0 137.9 %all-reduce.16.cloned.1.call-done = (f32[1152,864]{0,1:T(8,128)}, f32[144,3456]{1,0:T(8,128)}, f32[144,1152]{1,0:T(8,128)}, f32[144,4608]{1,0:T(8,128)}, f32[576,1152]{1,0:T(8,128)}) async-done(((f32[1152,864]{0,1:T(8,128)}, f32[144,3456]{1,0:T(8,128)}, f32[144,1152]{1,0:T(8,128)}, f32[144,4608]{1,0:T(8,128)}, f32[576,1152]{1,0:T(8,128)}), (f32[1152,864]{0,1:T(8,128)}, f32[144,3456]{1,0:T(8,128)}, ...) | async-done | bytes 11943952 | tf_op jit(solution)/shard_map/psum | solution.py:275
  2045.8 4.5 copy.95
  (210 shorter events, 46.4 us)
Async XLA Ops:
  7.2 50.2 %copy-start = (bf16[1152,864]{0,1:T(8,128)(2,1)S(1)}, bf16[1152,864]{0,1:T(8,128)(2,1)}, u32[]{:S(2)}) copy-start(bf16[1152,864]{0,1:T(8,128)(2,1)} %param.17) | copy-start | bytes 5971972
  7.2 2.9 copy-start.38
  7.2 6.1 copy-start.34
  7.2 6.8 copy-start.2
  7.2 126.8 %all-gather.5.cloned.1.call-start = ((), (), s32[]{:S(2)}) async-start(), calls=%async_computation.4 | async-start | bytes 8957952 | tf_op jit(solution)/shard_map/all_gather | solution.py:168
  8.0 181.5 %all-gather.7.cloned.1.call-start = ((), (), s32[]{:S(2)}) async-start(), calls=%async_computation.5 | async-start | bytes 2985984 | tf_op jit(solution)/shard_map/all_gather | solution.py:169
  8.7 6.1 copy-start.42
  8.7 6.3 copy-start.43
  8.7 6.6 copy-start.39
  8.7 6.8 copy-start.41
  8.8 334.0 %all-gather.9.cloned.1.call-start = ((), (), s32[]{:S(2)}) async-start(), calls=%async_computation.6 | async-start | bytes 11943936 | tf_op jit(solution)/shard_map/all_gather | solution.py:170
  9.5 486.0 %all-gather.11.cloned.1.call-start = ((), (), s32[]{:S(2)}) async-start(), calls=%async_computation.7 | async-start | bytes 11943936 | tf_op jit(solution)/shard_map/all_gather | solution.py:186
  10.1 47.9 %copy-start.40 = (bf16[864]{0:T(1024)(128)(2,1)S(1)}, bf16[864]{0:T(1024)(128)(2,1)}, u32[]{:S(2)}) copy-start(bf16[864]{0:T(1024)(128)(2,1)} %param.18) | copy-start | bytes 5188
  10.1 1146.4 %reduce-scatter.7.cloned.1.call-start = ((), (), s32[]{:S(2)}) async-start(), calls=%async_computation.9 | async-start | bytes 5971968 | tf_op jit(solution)/shard_map/reduce_scatter | solution.py:260
  13.4 79.5 %copy-start.25 = (f32[1152]{0:T(1024)}, f32[1152]{0:T(1024)S(1)}, u32[]{:S(2)}) copy-start(f32[1152]{0:T(1024)S(1)} %reduce.4) | copy-start | bytes 13828
  14.7 79.7 %copy-start.27 = (f32[512]{0:T(512)}, f32[512]{0:T(512)S(1)}, u32[]{:S(2)}) copy-start(f32[512]{0:T(512)S(1)} %rsqrt.27) | copy-start | bytes 6148
  14.8 79.7 %copy-start.29 = (f32[1,2,2,128]{3,1,2,0:T(2,128)}, f32[1,2,2,128]{3,1,2,0:T(2,128)S(1)}, u32[]{:S(2)}) copy-start(f32[1,2,2,128]{3,1,2,0:T(2,128)S(1)} %copy.73) | copy-start | bytes 6148
  57.2 38.8 %copy-start.36 = (f32[2]{0:T(128)}, f32[2]{0:T(128)S(1)}, u32[]{:S(2)}) copy-start(f32[2]{0:T(128)S(1)} %compare_convert_fusion) | copy-start | bytes 28
  179.2 3.3 copy-start.1
  179.2 3.3 copy-start.14
  495.5 18.0 copy-start.4
  513.5 12.3 copy-start.44
  534.6 621.8 %reduce-scatter.5.cloned.1.call-start = ((), (), s32[]{:S(2)}) async-start(), calls=%async_computation.8 | async-start | bytes 17915904 | tf_op jit(solution)/shard_map/reduce_scatter | solution.py:259
  551.0 14.2 slice-start
  557.7 4.9 copy-start.11
  557.7 7.6 slice-start.1
  582.3 898.2 %reduce-scatter.9.cloned.1.call-start = ((), (), s32[]{:S(2)}) async-start(), calls=%async_computation.10 | async-start | bytes 23887872 | tf_op jit(solution)/shard_map/reduce_scatter | solution.py:261
  595.5 1234.8 %reduce-scatter.11.cloned.1.call-start = ((), (), s32[]{:S(2)}) async-start(), calls=%async_computation.11 | async-start | bytes 23887872 | tf_op jit(solution)/shard_map/reduce_scatter | solution.py:262
  608.5 1437.4 %all-reduce.16.cloned.1.call-start = ((), (), s32[]{:S(2)}) async-start(), calls=%async_computation.12 | async-start | bytes 23887872 | tf_op jit(solution)/shard_map/psum | solution.py:275
  608.7 38.0 %collective-permute-start = (bf16[1,576,1152]{2,1,0:T(8,128)(2,1)}, bf16[1,576,1152]{2,1,0:T(8,128)(2,1)}, u32[]{:S(2)}, u32[]{:S(2)}) collective-permute-start(bf16[1,576,1152]{2,1,0:T(8,128)(2,1)} %bitcast.149), channel_id=1, source_target_pairs={{0,1},{1,0},{2,3},{3,2},{4,5},{5,4},{6,7},{7,6},{8,9},{9,8},{10,11... | collective-permute-start | bytes 3981320 | tf_op jit(solution)/shard_map/ppermute | solution.py:21
  651.7 138.7 %collective-permute-start.1 = (bf16[2,576,1152]{2,1,0:T(8,128)(2,1)}, bf16[2,576,1152]{2,1,0:T(8,128)(2,1)}, u32[]{:S(2)}, u32[]{:S(2)}) collective-permute-start(bf16[2,576,1152]{2,1,0:T(8,128)(2,1)} %get-tuple-element.107), channel_id=1, source_target_pairs={{0,2},{1,3},{2,0},{3,1},{4,6},{5,7},{6,4},{7,5},{8,10},{9,11},{10,... | collective-permute-start | bytes 7962632 | tf_op jit(solution)/shard_map/ppermute | solution.py:21
  793.5 3.7 copy-start.35
  793.5 6.3 copy-start.37
  793.5 8.1 copy-start.30
  796.9 1033.4 %collective-permute-start.2 = (bf16[4,576,1152]{2,1,0:T(8,128)(2,1)}, bf16[4,576,1152]{2,1,0:T(8,128)(2,1)}, u32[]{:S(2)}, u32[]{:S(2)}) collective-permute-start(bf16[4,576,1152]{2,1,0:T(8,128)(2,1)} %bitcast.16), channel_id=1, source_target_pairs={{0,4},{1,5},{2,6},{3,7},{4,0},{5,1},{6,2},{7,3},{8,12},{9,13},{10,... | collective-permute-start | bytes 15925256 | tf_op jit(solution)/shard_map/ppermute | solution.py:21
  799.8 13.6 slice-start.2
  799.8 13.6 slice-start.5
  801.7 10.5 copy-start.33
  801.7 10.5 copy-start.28
  801.7 11.8 slice-start.3
  801.7 11.8 slice-start.4
  801.7 11.7 slice-start.6
  812.1 9.1 copy-start.12
  814.7 339.5 %copy-start.31 = (f32[1152]{0:T(1024)S(1)}, f32[1152]{0:T(1024)}, u32[]{:S(2)}) copy-start(f32[1152]{0:T(1024)} %get-tuple-element.92) | copy-start | bytes 13828
  1836.0 42.4 %copy-start.26 = (f32[1152]{0:T(1024)S(1)}, f32[1152]{0:T(1024)}, u32[]{:S(2)}) copy-start(f32[1152]{0:T(1024)} %copy-done.25) | copy-start | bytes 13828
  1891.4 4.5 copy-start.5
  2045.8 4.5 copy-start.20
  2050.3 2.9 copy-start.18
  (16 other events, 28.6 us)
Sparse Core Ops, SparseCore 0:
  10.2 123.7 all-gather.4
  136.2 53.2 all-gather.6
  191.7 151.0 all-gather.8
  344.8 150.6 all-gather.10
  534.7 107.2 reduce-scatter.6
  646.2 484.5 reduce-scatter.4
  1135.2 345.2 reduce-scatter.8
  1484.4 345.8 reduce-scatter.10
  1834.1 211.7 all-reduce.15
